TPU v7x, 128 devices: a whole 4x4x4 slice. The times are simulated.
128 devices in a mesh: gx: 16 (over x, y), gy: 8 (over z, core).
Axes of the slice: x: 4, y: 4, z: 4, core: 2. Of those that a mesh axis runs over, the one named last changes fastest.
Arguments:
- volts: float32 [32, 4, 128, 1024], P(None, None, 'gx', 'gy'), may hold values from -6 to 6
- cap: float32 [4, 128, 1024], P(None, 'gx', 'gy'), may hold values from 0.05 to 1
- cond_x: float32 [4, 128, 1024], P(None, 'gx', 'gy'), may hold values from 0.5 to 2
- cond_y: float32 [4, 128, 1024], P(None, 'gx', 'gy'), may hold values from 0.5 to 2
- via: float32 [4, 128, 1024], P(None, 'gx', 'gy'), may hold values from 0.2 to 2
- waveforms: float32 [64, 64], replicated, may hold values from -6 to 6
- placement: int32 [1048576, 1], P(('gx', 'gy')), may hold values from 0 to 127; in each aligned block of 8192 rows (0 to 8191, 8192 to 16383, ...) at most 128 rows name the same one
- cells: int32 [1048576], P(('gx', 'gy')), may hold values from 0 to 1023
- wave_ids: int32 [1048576], P(('gx', 'gy')), may hold values from 0 to 63
- amps: float32 [1048576], P(('gx', 'gy')), may hold values from 0.5 to 4
Outputs:
- volts_out: float32 [32, 4, 128, 1024], P(None, None, 'gx', 'gy')
- residual: float32 [32, 4, 128, 1024], P(None, None, 'gx', 'gy')
Inputs may be any that keep to these rules, and one draw needn't show every extreme that they name: `placement`: in each device's block of 8192 rows no tile is named more than 128 times, a bound that some block reaches.
All inputs are finite; a program needn't handle non-finite values.
Results may differ from a plain program's by a relative error of at most 0.0029.
Values may be sent and summed in bfloat16 or wider, within the bound.
No kernel may reach another device: no remote copies, remote signals or barrier semaphores. Data moves between devices by JAX's collectives and lax.ppermute only.
A program may use at most 64 MiB of HBM per device.

v0:
```python
import functools
import jax
import jax.numpy as jnp
from jax import lax
from jax.sharding import Mesh
from jax.sharding import PartitionSpec as P

ITERS = 3
GX_GY = ("gx_0", "gx_1", "gy_0", "gy_1")
GX = ("gx_0", "gx_1")
GY = ("gy_0", "gy_1")


def with_halo(x, sides, width):
    edges = {}
    for axis, dim in sides:
        size, length = (lax.axis_size(axis), x.shape[dim])
        up = [(i, (i + 1) % size) for i in range(size - 1)]
        last = lax.slice_in_dim(x, length - width, length, axis=dim)
        initial = lax.slice_in_dim(x, 0, width, axis=dim)
        edges[dim] = (
            lax.ppermute(last, axis, up),
            lax.ppermute(initial, axis, [(b, a) for a, b in up]),
        )
    done = []
    for _, dim in sides:
        low, high = edges[dim]
        around = [(width, width) if d in done else (0, 0) for d in range(x.ndim)]
        x = jnp.concatenate([jnp.pad(low, around), x, jnp.pad(high, around)], axis=dim)
        done.append(dim)
    return x


def shifted(x, axis, by):
    length = lax.axis_size(axis)
    pairs = [(i, i + by) for i in range(length) if 0 <= i + by < length]
    return lax.ppermute(x, axis, pairs)


def by_axis(x, axes):
    return functools.reduce(lax.psum, axes, x)


def gram(left, right):
    left_rows = left.reshape(left.shape[0], -1)
    right_rows = right.reshape(right.shape[0], -1)
    return lax.dot_general(
        left_rows, right_rows, (((1,), (1,)), ((), ())), precision=lax.Precision.HIGHEST
    )


def combine(coef, field):
    return jnp.einsum("st,slxy->tlxy", coef, field, precision=lax.Precision.HIGHEST)


def spd_solve(matrix, right):
    factor = jnp.linalg.cholesky(matrix)
    return jax.scipy.linalg.cho_solve((factor, True), right)


def make_currents(waveforms, kinds, scales):
    table_hits = (
        jnp.arange(waveforms.shape[1], dtype=jnp.int32)[:, None] == kinds[None, :]
    ).astype(jnp.float32)
    picked = jnp.dot(waveforms, table_hits, precision=lax.Precision.HIGHEST)
    return (picked * scales[None, :]).astype(jnp.bfloat16)


def operate(field, cap, cond_x, cond_x_low, cond_y, cond_y_low, via, via_low):
    padded = with_halo(field, ((GX, 2), (GY, 3)), 1)
    zero_layer = jnp.zeros_like(field[:, :1])
    upper = jnp.concatenate([field[:, 1:], zero_layer], axis=1)
    lower = jnp.concatenate([zero_layer, field[:, :-1]], axis=1)
    result = cap * field
    result = result + cond_x * (field - padded[:, :, 2:, 1:-1])
    result = result + cond_x_low * (field - padded[:, :, :-2, 1:-1])
    result = result + cond_y * (field - padded[:, :, 1:-1, 2:])
    result = result + cond_y_low * (field - padded[:, :, 1:-1, :-2])
    result = result + via * (field - upper) + via_low * (field - lower)
    return result


def body(volts, cap, cond_x, cond_y, via, waveforms, placement, cells, wave_ids, amps):
    devices = lax.axis_size(GX_GY)
    scenarios = volts.shape[0]
    steps = waveforms.shape[0] // scenarios
    tile_x = volts.shape[2]
    tile_y = volts.shape[3]
    die_cells = tile_x * tile_y
    slots_all = 2 * cells.shape[0]
    capacity = slots_all // devices
    target = placement[:, 0]
    target_hits = (jnp.arange(devices, dtype=jnp.int32)[:, None] == target[None, :]).astype(
        jnp.int32
    )
    running = jnp.cumsum(target_hits, axis=1) - 1
    position = jnp.sum(target_hits * running, axis=0)
    slot_index = target * capacity + position
    currents = make_currents(waveforms, wave_ids, amps)
    packed = jnp.zeros((currents.shape[0], slots_all), jnp.bfloat16).at[:, slot_index].set(currents)
    cell_slots = jnp.zeros((1, slots_all), jnp.int32).at[0, slot_index].set(cells)
    arrived, cell_slots = (
        lax.all_to_all(packed, GX_GY, split_axis=1, concat_axis=1, tiled=True),
        lax.all_to_all(cell_slots, GX_GY, split_axis=1, concat_axis=1, tiled=True),
    )
    block_rows = min(1024, slots_all)
    block_count = slots_all // block_rows
    cell_line = jnp.arange(die_cells, dtype=jnp.int32)

    def add_block(turn, total):
        piece_values = lax.dynamic_slice_in_dim(arrived, turn * block_rows, block_rows, 1)
        piece_cells = lax.dynamic_slice_in_dim(cell_slots[0], turn * block_rows, block_rows, 0)
        one_hot = (piece_cells[:, None] == cell_line[None, :]).astype(jnp.bfloat16)
        return total + jnp.dot(piece_values, one_hot, preferred_element_type=jnp.float32)

    injected = lax.fori_loop(
        0, block_count, add_block, jnp.zeros((arrived.shape[0], die_cells), jnp.float32)
    )
    injected = injected.reshape(steps, scenarios, tile_x, tile_y)
    rim_x = shifted(cond_x[:, -1:, :], GX, 1)
    rim_y = shifted(cond_y[:, :, -1:], GY, 1)
    cond_x_low = jnp.concatenate([rim_x, cond_x[:, :-1, :]], axis=1)
    cond_y_low = jnp.concatenate([rim_y, cond_y[:, :, :-1]], axis=2)
    via_low = jnp.concatenate([jnp.zeros_like(via[:1]), via[:-1]], axis=0)

    def apply_grid(field):
        return operate(field, cap, cond_x, cond_x_low, cond_y, cond_y_low, via, via_low)

    voltage = volts
    residual = volts
    for step in range(steps):
        rhs = cap * voltage
        rhs = rhs.at[:, 0].add(-injected[step])
        iterate = voltage
        residual = rhs - apply_grid(iterate)
        direction = residual
        norm_gram = by_axis(gram(residual, residual), GX_GY)
        for sweep in range(ITERS):
            image = apply_grid(direction)
            curve_gram, cross_gram, image_gram = (
                by_axis(gram(direction, image), GX_GY),
                by_axis(gram(residual, image), GX_GY),
                by_axis(gram(image, image), GX_GY),
            )
            step_coef = spd_solve(curve_gram, norm_gram)
            iterate = iterate + combine(step_coef, direction)
            residual = residual - combine(step_coef, image)
            if sweep + 1 < ITERS:
                cross_term = jnp.dot(cross_gram, step_coef, precision=lax.Precision.HIGHEST)
                square_term = jnp.dot(
                    step_coef.T,
                    jnp.dot(image_gram, step_coef, precision=lax.Precision.HIGHEST),
                    precision=lax.Precision.HIGHEST,
                )
                new_gram = norm_gram - cross_term - cross_term.T + square_term
                turn_coef = spd_solve(norm_gram, new_gram)
                direction = residual + combine(turn_coef, direction)
                norm_gram = new_gram
        voltage = iterate
    return (voltage, residual)


def solution(mesh):
    finer = Mesh(mesh.devices.reshape(4, 4, 4, 2), ("gx_0", "gx_1", "gy_0", "gy_1"))
    in_specs = (
        P(None, None, GX, GY),
        P(None, GX, GY),
        P(None, GX, GY),
        P(None, GX, GY),
        P(None, GX, GY),
        P(),
        P(GX_GY, None),
        P(GX_GY),
        P(GX_GY),
        P(GX_GY),
    )
    out_specs = (P(None, None, GX, GY), P(None, None, GX, GY))
    return jax.shard_map(body, mesh=finer, in_specs=in_specs, out_specs=out_specs, check_vma=False)
```

profile of v0, /device:TPU:1, one launch (start us, length us, event | category | flops | bytes accessed | tf_op | source)
XLA Modules:
  0.0 691.4 jit_solution(8659340981578746071)
XLA Ops:
  4.7 5.3 select_reduce_fusion
  12.3 23.6 %scatter_custom_fusion = bf16[64,16384]{0,1:T(8,128)(2,1)} fusion(s32[8192]{0:T(1024)S(1)} %bitcast.343, bf16[8192,64]{1,0:T(8,128)(2,1)S(1)} %copy.198, bf16[]{:T(256)} %constant.131.clone.1), kind=kCustom, calls=%fused_computation.19 | custom fusion | bytes 2097154 | tf_op jit(solution)/shard_map/scatter | solution.py:100
  36.0 4.8 copy.199
  40.8 11.5 %all-to-all-start = ((bf16[64,128,128]{2,0,1:T(8,128)(2,1)}), bf16[64,128,128]{2,0,1:T(8,128)(2,1)S(1)}, u32[]{:S(2)}, u32[]{:S(2)}) async-start(bf16[64,128,128]{2,0,1:T(8,128)(2,1)} %copy.199), calls=%async_computation | async-start | bytes 4194304 | tf_op jit(solution)/shard_map/all_to_all | solution.py:103
  58.6 3.8 collective-permute-start.4
  62.4 4.3 collective-permute-start.1
  70.1 31.2 %scatter_custom_fusion.1 = s32[16384]{0:T(1024)} fusion(s32[8192]{0:T(1024)S(1)} %broadcast_select_fusion, s32[8192]{0:T(1024)} %param.26, s32[]{:T(128)} %constant.129.clone.1), kind=kCustom, calls=%fused_computation.288 | custom fusion | bytes 66048
  102.4 3.6 collective-permute-start.5
  109.4 10.8 %all-to-all-start.1 = ((s32[1,128,128]{2,0,1:T(1,128)}), s32[1,128,128]{2,0,1:T(1,128)S(1)}, u32[]{:S(2)}, u32[]{:S(2)}) async-start(s32[1,128,128]{2,0,1:T(1,128)} %bitcast.5), calls=%async_computation.1 | async-start | bytes 131072 | tf_op jit(solution)/shard_map/all_to_all | solution.py:104
  121.8 7.7 %all-to-all-done.1 = s32[1,128,128]{2,0,1:T(1,128)S(1)} async-done(((s32[1,128,128]{2,0,1:T(1,128)}), s32[1,128,128]{2,0,1:T(1,128)S(1)}, u32[]{:S(2)}, u32[]{:S(2)}) %all-to-all-start.1) | async-done | bytes 65568 | tf_op jit(solution)/shard_map/all_to_all | solution.py:104
  129.6 43.1 %while.16 = (s32[]{:T(128)}, f32[64,1024]{1,0:T(8,128)}, bf16[64,16384]{1,0:T(8,128)(2,1)}, s32[1,16384]{1,0:T(1,128)S(1)}, s32[]{:T(128)}, /*index=5*/s32[]{:T(128)}, s32[]{:T(128)}, s32[]{:T(128)}) while((s32[]{:T(128)}, f32[64,1024]{1,0:T(8,128)}, bf16[64,16384]{1,0:T(8,128)(2,1)}, s32[1,16384]{1,0:T(1,128)S(1)}, s32[]{:T(128)}, ...), condition=%wide.region_6.7_spmd.clone, body=%wide.region_5.6_spmd.clone.sunk | while | flops 135397376 | bytes 667797 | solution.py:116
  183.2 4.0 collective-permute-start.7
  190.3 16.8 %all-reduce.45 = (f32[32,32]{0,1:T(8,128)S(1)}, f32[32,32]{0,1:T(8,128)S(1)}, f32[32,32]{1,0:T(8,128)S(1)}) all-reduce(f32[32,32]{0,1:T(8,128)S(1)} %convolution_bitcast_fusion.18, f32[32,32]{0,1:T(8,128)S(1)} %convolution_bitcast_fusion.19, ...), channel_id=1, replica_groups=mesh['gx_0'=4,'gx_1'=4,'gy_0'=4,'gy_1'=2] {'gx_0'}, use_global_device_ids=true, to_apply=%region_13.15 | all-reduce | flops 3072 | bytes 24576 | tf_op jit(solution)/shard_map/psum | solution.py:41
  207.1 11.2 %all-reduce.41 = (f32[32,32]{0,1:T(8,128)S(1)}, f32[32,32]{0,1:T(8,128)S(1)}, f32[32,32]{1,0:T(8,128)S(1)}) all-reduce(f32[32,32]{0,1:T(8,128)S(1)} %get-tuple-element.189, f32[32,32]{0,1:T(8,128)S(1)} %get-tuple-element.190, f32[32,32]{1,0:T(8,128)S(1)} %get-tuple-element.191), channel_id=1, replica_groups=mesh['gx_0'=4,'gx_1'=4,'gy_0'=4,'gy_1'=2] {'gx_1'}, use_global_device_ids=true, to_apply=%region_14.16 | all-reduce | flops 3072 | bytes 24576 | tf_op jit(solution)/shard_map/psum | solution.py:41
  218.3 11.7 %all-reduce.37 = (f32[32,32]{0,1:T(8,128)S(1)}, f32[32,32]{0,1:T(8,128)S(1)}, f32[32,32]{1,0:T(8,128)S(1)}) all-reduce(f32[32,32]{0,1:T(8,128)S(1)} %get-tuple-element.177, f32[32,32]{0,1:T(8,128)S(1)} %get-tuple-element.178, f32[32,32]{1,0:T(8,128)S(1)} %get-tuple-element.179), channel_id=1, replica_groups=mesh['gx_0'=4,'gx_1'=4,'gy_0'=4,'gy_1'=2] {'gy_0'}, use_global_device_ids=true, to_apply=%region_15.17 | all-reduce | flops 3072 | bytes 24576 | tf_op jit(solution)/shard_map/psum | solution.py:41
  230.0 15.0 %all-reduce.49 = (f32[32,32]{0,1:T(8,128)S(1)}, f32[32,32]{0,1:T(8,128)S(1)}, f32[32,32]{1,0:T(8,128)S(1)}) all-reduce(f32[32,32]{0,1:T(8,128)S(1)} %get-tuple-element.165, f32[32,32]{0,1:T(8,128)S(1)} %get-tuple-element.166, f32[32,32]{1,0:T(8,128)S(1)} %get-tuple-element.167), channel_id=1, replica_groups=mesh['gx_0'=4,'gx_1'=4,'gy_0'=4,'gy_1'=2] {'gy_1'}, use_global_device_ids=true, to_apply=%region_16.18 | all-reduce | flops 3072 | bytes 24576 | tf_op jit(solution)/shard_map/psum | solution.py:41
  271.9 3.5 collective-permute-start.13
  276.7 4.2 collective-permute-start.11
  288.2 14.5 %all-reduce.44 = (f32[32,32]{0,1:T(8,128)S(1)}, f32[32,32]{1,0:T(8,128)S(1)}, f32[32,32]{1,0:T(8,128)S(1)}) all-reduce(f32[32,32]{0,1:T(8,128)S(1)} %convolution_bitcast_fusion.15, f32[32,32]{1,0:T(8,128)S(1)} %convolution_bitcast_fusion.13, ...), channel_id=1, replica_groups=mesh['gx_0'=4,'gx_1'=4,'gy_0'=4,'gy_1'=2] {'gx_0'}, use_global_device_ids=true, to_apply=%region_21.24 | all-reduce | flops 3072 | bytes 24576 | tf_op jit(solution)/shard_map/psum | solution.py:41
  302.7 11.6 %all-reduce.40 = (f32[32,32]{0,1:T(8,128)S(1)}, f32[32,32]{1,0:T(8,128)S(1)}, f32[32,32]{1,0:T(8,128)S(1)}) all-reduce(f32[32,32]{0,1:T(8,128)S(1)} %get-tuple-element.186, f32[32,32]{1,0:T(8,128)S(1)} %get-tuple-element.187, f32[32,32]{1,0:T(8,128)S(1)} %get-tuple-element.188), channel_id=1, replica_groups=mesh['gx_0'=4,'gx_1'=4,'gy_0'=4,'gy_1'=2] {'gx_1'}, use_global_device_ids=true, to_apply=%region_22.25 | all-reduce | flops 3072 | bytes 24576 | tf_op jit(solution)/shard_map/psum | solution.py:41
  314.4 11.2 %all-reduce.36 = (f32[32,32]{0,1:T(8,128)S(1)}, f32[32,32]{1,0:T(8,128)S(1)}, f32[32,32]{1,0:T(8,128)S(1)}) all-reduce(f32[32,32]{0,1:T(8,128)S(1)} %get-tuple-element.174, f32[32,32]{1,0:T(8,128)S(1)} %get-tuple-element.175, f32[32,32]{1,0:T(8,128)S(1)} %get-tuple-element.176), channel_id=1, replica_groups=mesh['gx_0'=4,'gx_1'=4,'gy_0'=4,'gy_1'=2] {'gy_0'}, use_global_device_ids=true, to_apply=%region_23.26 | all-reduce | flops 3072 | bytes 24576 | tf_op jit(solution)/shard_map/psum | solution.py:41
  325.6 15.0 %all-reduce.48 = (f32[32,32]{0,1:T(8,128)S(1)}, f32[32,32]{1,0:T(8,128)S(1)}, f32[32,32]{1,0:T(8,128)S(1)}) all-reduce(f32[32,32]{0,1:T(8,128)S(1)} %get-tuple-element.162, f32[32,32]{1,0:T(8,128)S(1)} %get-tuple-element.163, f32[32,32]{1,0:T(8,128)S(1)} %get-tuple-element.164), channel_id=1, replica_groups=mesh['gx_0'=4,'gx_1'=4,'gy_0'=4,'gy_1'=2] {'gy_1'}, use_global_device_ids=true, to_apply=%region_24.27 | all-reduce | flops 3072 | bytes 24576 | tf_op jit(solution)/shard_map/psum | solution.py:41
  352.4 3.5 collective-permute-start.17
  357.2 4.0 collective-permute-start.15
  363.9 16.0 %psum.440 = f32[32,32]{0,1:T(8,128)S(1)} all-reduce(f32[32,32]{0,1:T(8,128)S(1)} %convolution_bitcast_fusion.11), channel_id=1, replica_groups=mesh['gx_0'=4,'gx_1'=4,'gy_0'=4,'gy_1'=2] {'gx_0'}, use_global_device_ids=true, to_apply=%region_33.36 | all-reduce | flops 1024 | bytes 8192 | tf_op jit(solution)/shard_map/psum | solution.py:41
  379.9 10.8 %psum.441 = f32[32,32]{0,1:T(8,128)S(1)} all-reduce(f32[32,32]{0,1:T(8,128)S(1)} %psum.440), channel_id=1, replica_groups=mesh['gx_0'=4,'gx_1'=4,'gy_0'=4,'gy_1'=2] {'gx_1'}, use_global_device_ids=true, to_apply=%region_34.37 | all-reduce | flops 1024 | bytes 8192 | tf_op jit(solution)/shard_map/psum | solution.py:41
  390.7 10.8 %psum.442 = f32[32,32]{0,1:T(8,128)S(1)} all-reduce(f32[32,32]{0,1:T(8,128)S(1)} %psum.441), channel_id=1, replica_groups=mesh['gx_0'=4,'gx_1'=4,'gy_0'=4,'gy_1'=2] {'gy_0'}, use_global_device_ids=true, to_apply=%region_35.38 | all-reduce | flops 1024 | bytes 8192 | tf_op jit(solution)/shard_map/psum | solution.py:41
  401.4 15.2 %psum.443 = f32[32,32]{0,1:T(8,128)S(1)} all-reduce(f32[32,32]{0,1:T(8,128)S(1)} %psum.442), channel_id=1, replica_groups=mesh['gx_0'=4,'gx_1'=4,'gy_0'=4,'gy_1'=2] {'gy_1'}, use_global_device_ids=true, to_apply=%region_36.39 | all-reduce | flops 1024 | bytes 8192 | tf_op jit(solution)/shard_map/psum | solution.py:41
  426.9 3.5 collective-permute-start.21
  431.7 4.4 collective-permute-start.19
  440.3 3.6 collective-permute-start.25
  445.1 4.4 collective-permute-start.23
  452.9 18.1 %all-reduce.43 = (f32[32,32]{0,1:T(8,128)S(1)}, f32[32,32]{0,1:T(8,128)S(1)}, f32[32,32]{1,0:T(8,128)S(1)}) all-reduce(f32[32,32]{0,1:T(8,128)S(1)} %convolution_bitcast_fusion.8, f32[32,32]{0,1:T(8,128)S(1)} %convolution_bitcast_fusion.9, ...), channel_id=1, replica_groups=mesh['gx_0'=4,'gx_1'=4,'gy_0'=4,'gy_1'=2] {'gx_0'}, use_global_device_ids=true, to_apply=%region_41.44 | all-reduce | flops 3072 | bytes 24576 | tf_op jit(solution)/shard_map/psum | solution.py:41
  471.0 11.2 %all-reduce.39 = (f32[32,32]{0,1:T(8,128)S(1)}, f32[32,32]{0,1:T(8,128)S(1)}, f32[32,32]{1,0:T(8,128)S(1)}) all-reduce(f32[32,32]{0,1:T(8,128)S(1)} %get-tuple-element.183, f32[32,32]{0,1:T(8,128)S(1)} %get-tuple-element.184, f32[32,32]{1,0:T(8,128)S(1)} %get-tuple-element.185), channel_id=1, replica_groups=mesh['gx_0'=4,'gx_1'=4,'gy_0'=4,'gy_1'=2] {'gx_1'}, use_global_device_ids=true, to_apply=%region_42.45 | all-reduce | flops 3072 | bytes 24576 | tf_op jit(solution)/shard_map/psum | solution.py:41
  482.3 11.2 %all-reduce.35 = (f32[32,32]{0,1:T(8,128)S(1)}, f32[32,32]{0,1:T(8,128)S(1)}, f32[32,32]{1,0:T(8,128)S(1)}) all-reduce(f32[32,32]{0,1:T(8,128)S(1)} %get-tuple-element.171, f32[32,32]{0,1:T(8,128)S(1)} %get-tuple-element.172, f32[32,32]{1,0:T(8,128)S(1)} %get-tuple-element.173), channel_id=1, replica_groups=mesh['gx_0'=4,'gx_1'=4,'gy_0'=4,'gy_1'=2] {'gy_0'}, use_global_device_ids=true, to_apply=%region_43.46 | all-reduce | flops 3072 | bytes 24576 | tf_op jit(solution)/shard_map/psum | solution.py:41
  493.5 15.2 %all-reduce.47 = (f32[32,32]{0,1:T(8,128)S(1)}, f32[32,32]{0,1:T(8,128)S(1)}, f32[32,32]{1,0:T(8,128)S(1)}) all-reduce(f32[32,32]{0,1:T(8,128)S(1)} %get-tuple-element.159, f32[32,32]{0,1:T(8,128)S(1)} %get-tuple-element.160, f32[32,32]{1,0:T(8,128)S(1)} %get-tuple-element.161), channel_id=1, replica_groups=mesh['gx_0'=4,'gx_1'=4,'gy_0'=4,'gy_1'=2] {'gy_1'}, use_global_device_ids=true, to_apply=%region_44.47 | all-reduce | flops 3072 | bytes 24576 | tf_op jit(solution)/shard_map/psum | solution.py:41
  535.5 3.5 collective-permute-start.29
  540.3 4.0 collective-permute-start.27
  552.3 14.3 %all-reduce.42 = (f32[32,32]{0,1:T(8,128)S(1)}, f32[32,32]{1,0:T(8,128)S(1)}, f32[32,32]{1,0:T(8,128)S(1)}) all-reduce(f32[32,32]{0,1:T(8,128)S(1)} %convolution_bitcast_fusion.5, f32[32,32]{1,0:T(8,128)S(1)} %convolution_bitcast_fusion.3, ...), channel_id=1, replica_groups=mesh['gx_0'=4,'gx_1'=4,'gy_0'=4,'gy_1'=2] {'gx_0'}, use_global_device_ids=true, to_apply=%region_49.52 | all-reduce | flops 3072 | bytes 24576 | tf_op jit(solution)/shard_map/psum | solution.py:41
  566.6 12.1 %all-reduce.38 = (f32[32,32]{0,1:T(8,128)S(1)}, f32[32,32]{1,0:T(8,128)S(1)}, f32[32,32]{1,0:T(8,128)S(1)}) all-reduce(f32[32,32]{0,1:T(8,128)S(1)} %get-tuple-element.180, f32[32,32]{1,0:T(8,128)S(1)} %get-tuple-element.181, f32[32,32]{1,0:T(8,128)S(1)} %get-tuple-element.182), channel_id=1, replica_groups=mesh['gx_0'=4,'gx_1'=4,'gy_0'=4,'gy_1'=2] {'gx_1'}, use_global_device_ids=true, to_apply=%region_50.53 | all-reduce | flops 3072 | bytes 24576 | tf_op jit(solution)/shard_map/psum | solution.py:41
  578.7 11.2 %all-reduce.34 = (f32[32,32]{0,1:T(8,128)S(1)}, f32[32,32]{1,0:T(8,128)S(1)}, f32[32,32]{1,0:T(8,128)S(1)}) all-reduce(f32[32,32]{0,1:T(8,128)S(1)} %get-tuple-element.168, f32[32,32]{1,0:T(8,128)S(1)} %get-tuple-element.169, f32[32,32]{1,0:T(8,128)S(1)} %get-tuple-element.170), channel_id=1, replica_groups=mesh['gx_0'=4,'gx_1'=4,'gy_0'=4,'gy_1'=2] {'gy_0'}, use_global_device_ids=true, to_apply=%region_51.54 | all-reduce | flops 3072 | bytes 24576 | tf_op jit(solution)/shard_map/psum | solution.py:41
  590.0 15.0 %all-reduce.46 = (f32[32,32]{0,1:T(8,128)S(1)}, f32[32,32]{1,0:T(8,128)S(1)}, f32[32,32]{1,0:T(8,128)S(1)}) all-reduce(f32[32,32]{0,1:T(8,128)S(1)} %get-tuple-element.156, f32[32,32]{1,0:T(8,128)S(1)} %get-tuple-element.157, f32[32,32]{1,0:T(8,128)S(1)} %get-tuple-element.158), channel_id=1, replica_groups=mesh['gx_0'=4,'gx_1'=4,'gy_0'=4,'gy_1'=2] {'gy_1'}, use_global_device_ids=true, to_apply=%region_52.55 | all-reduce | flops 3072 | bytes 24576 | tf_op jit(solution)/shard_map/psum | solution.py:41
  616.7 3.5 collective-permute-start.33
  621.5 4.0 collective-permute-start.31
  628.4 15.4 %psum.468 = f32[32,32]{0,1:T(8,128)S(1)} all-reduce(f32[32,32]{0,1:T(8,128)S(1)} %convolution_bitcast_fusion.1), channel_id=1, replica_groups=mesh['gx_0'=4,'gx_1'=4,'gy_0'=4,'gy_1'=2] {'gx_0'}, use_global_device_ids=true, to_apply=%region_61.64 | all-reduce | flops 1024 | bytes 8192 | tf_op jit(solution)/shard_map/psum | solution.py:41
  643.8 10.8 %psum.469 = f32[32,32]{0,1:T(8,128)S(1)} all-reduce(f32[32,32]{0,1:T(8,128)S(1)} %psum.468), channel_id=1, replica_groups=mesh['gx_0'=4,'gx_1'=4,'gy_0'=4,'gy_1'=2] {'gx_1'}, use_global_device_ids=true, to_apply=%region_62.65 | all-reduce | flops 1024 | bytes 8192 | tf_op jit(solution)/shard_map/psum | solution.py:41
  654.6 10.8 %psum.470 = f32[32,32]{0,1:T(8,128)S(1)} all-reduce(f32[32,32]{0,1:T(8,128)S(1)} %psum.469), channel_id=1, replica_groups=mesh['gx_0'=4,'gx_1'=4,'gy_0'=4,'gy_1'=2] {'gy_0'}, use_global_device_ids=true, to_apply=%region_63.66 | all-reduce | flops 1024 | bytes 8192 | tf_op jit(solution)/shard_map/psum | solution.py:41
  665.4 15.2 %psum.471 = f32[32,32]{0,1:T(8,128)S(1)} all-reduce(f32[32,32]{0,1:T(8,128)S(1)} %psum.470), channel_id=1, replica_groups=mesh['gx_0'=4,'gx_1'=4,'gy_0'=4,'gy_1'=2] {'gy_1'}, use_global_device_ids=true, to_apply=%region_64.67 | all-reduce | flops 1024 | bytes 8192 | tf_op jit(solution)/shard_map/psum | solution.py:41
  (338 shorter events, 211.8 us)
Async XLA Ops:
  40.8 29.1 %copy-start.25 = (s32[2]{0:T(128)S(1)}, s32[2]{0:T(128)}, u32[]{:S(2)}) copy-start(s32[2]{0:T(128)} %constant.211) | copy-start | bytes 28
  40.8 61.5 %slice-start = ((f32[4,8,128]{2,1,0:T(8,128)}), f32[3,8,128]{2,1,0:T(8,128)S(1)}, s32[]{:S(2)}) async-start(f32[4,8,128]{2,1,0:T(8,128)} %param.23), calls=%async_computation.2 | async-start | bytes 24576 | tf_op jit(solution)/shard_map/slice | solution.py:124
  40.8 66.6 %copy-start.6 = (f32[4,8,128]{2,1,0:T(8,128)S(1)}, f32[4,8,128]{2,1,0:T(8,128)}, u32[]{:S(2)}) copy-start(f32[4,8,128]{2,1,0:T(8,128)} %param.20) | copy-start | bytes 49156
  40.8 68.6 %all-to-all-start = ((bf16[64,128,128]{2,0,1:T(8,128)(2,1)}), bf16[64,128,128]{2,0,1:T(8,128)(2,1)S(1)}, u32[]{:S(2)}, u32[]{:S(2)}) async-start(bf16[64,128,128]{2,0,1:T(8,128)(2,1)} %copy.199), calls=%async_computation | async-start | bytes 4194304 | tf_op jit(solution)/shard_map/all_to_all | solution.py:103
  53.3 53.5 %collective-permute-start.2 = (f32[32,4,1,128]{3,0,2,1:T(8,128)}, f32[32,4,1,128]{3,0,2,1:T(8,128)S(1)}, u32[]{:S(2)}, u32[]{:S(2)}) collective-permute-start(f32[32,4,1,128]{3,0,2,1:T(8,128)} %get-tuple-element.251), channel_id=1, source_target_pairs={{0,8},{8,16},{16,24},{24,32},{32,40},{40,48},{48,56},{56,64},{64,7... | collective-permute-start | bytes 196616 | tf_op jit(solution)/shard_map/ppermute | solution.py:22
  56.6 52.2 %collective-permute-start = (f32[32,4,1,128]{3,0,2,1:T(8,128)S(1)}, f32[32,4,1,128]{3,0,2,1:T(8,128)S(1)}, u32[]{:S(2)}, u32[]{:S(2)}) collective-permute-start(f32[32,4,1,128]{3,0,2,1:T(8,128)S(1)} %get-tuple-element.250), channel_id=1, source_target_pairs={{8,0},{16,8},{24,16},{32,24},{40,32},{48,40},{56,48},{64,56},{72,6... | collective-permute-start | bytes 196616 | tf_op jit(solution)/shard_map/ppermute | solution.py:23
  58.6 43.8 %collective-permute-start.4 = (f32[4,8,1]{2,1,0:T(8,128)}, f32[4,8,1]{2,1,0:T(8,128)}, u32[]{:S(2)}, u32[]{:S(2)}) collective-permute-start(f32[4,8,1]{2,1,0:T(8,128)} %slice.379), channel_id=1, source_target_pairs={{0,1},{1,2},{2,3},{3,4},{4,5},{5,6},{6,7},{8,9},{9,10},{10,11},{11... | collective-permute-start | bytes 392 | tf_op jit(solution)/shard_map/ppermute | solution.py:37
  62.4 44.4 %collective-permute-start.1 = (f32[4,1,128]{2,1,0:T(1,128)S(1)}, f32[4,1,128]{2,1,0:T(1,128)S(1)}, u32[]{:S(2)}, u32[]{:S(2)}) collective-permute-start(f32[4,1,128]{2,1,0:T(1,128)S(1)} %slice.373), channel_id=1, source_target_pairs={{0,8},{8,16},{16,24},{24,32},{32,40},{40,48},{48,56},{56,64},{64,7... | collective-permute-start | bytes 6152 | tf_op jit(solution)/shard_map/ppermute | solution.py:37
  67.8 105.9 %collective-permute-start.3 = (f32[32,4,8,1]{3,0,2,1:T(8,128)}, f32[32,4,8,1]{3,0,2,1:T(8,128)}, u32[]{:S(2)}, u32[]{:S(2)}) collective-permute-start(f32[32,4,8,1]{3,0,2,1:T(8,128)} %get-tuple-element.248), channel_id=1, source_target_pairs={{1,0},{2,1},{3,2},{4,3},{5,4},{6,5},{7,6},{9,8},{10,9},{11,10},{12... | collective-permute-start | bytes 12296 | tf_op jit(solution)/shard_map/ppermute | solution.py:23
  102.4 71.4 %collective-permute-start.5 = (f32[32,4,8,1]{3,0,2,1:T(8,128)}, f32[32,4,8,1]{3,0,2,1:T(8,128)}, u32[]{:S(2)}, u32[]{:S(2)}) collective-permute-start(f32[32,4,8,1]{3,0,2,1:T(8,128)} %get-tuple-element.249), channel_id=1, source_target_pairs={{0,1},{1,2},{2,3},{3,4},{4,5},{5,6},{6,7},{8,9},{9,10},{10,11},{11... | collective-permute-start | bytes 12296 | tf_op jit(solution)/shard_map/ppermute | solution.py:22
  109.4 20.2 %all-to-all-start.1 = ((s32[1,128,128]{2,0,1:T(1,128)}), s32[1,128,128]{2,0,1:T(1,128)S(1)}, u32[]{:S(2)}, u32[]{:S(2)}) async-start(s32[1,128,128]{2,0,1:T(1,128)} %bitcast.5), calls=%async_computation.1 | async-start | bytes 131072 | tf_op jit(solution)/shard_map/all_to_all | solution.py:104
  129.6 44.1 %copy-start.3 = (f32[32,4,8,128]{3,0,2,1:T(8,128)S(1)}, f32[32,4,8,128]{3,0,2,1:T(8,128)}, u32[]{:S(2)}) copy-start(f32[32,4,8,128]{3,0,2,1:T(8,128)} %get-tuple-element.253) | copy-start | bytes 1572868
  129.6 44.2 %copy-start.4 = (f32[32,3,8,128]{3,0,2,1:T(8,128)S(1)}, f32[32,3,8,128]{3,0,2,1:T(8,128)}, u32[]{:S(2)}) copy-start(f32[32,3,8,128]{3,0,2,1:T(8,128)} %get-tuple-element.246) | copy-start | bytes 1179652
  129.6 44.2 %copy-start.5 = (f32[32,3,8,128]{3,0,2,1:T(8,128)S(1)}, f32[32,3,8,128]{3,0,2,1:T(8,128)}, u32[]{:S(2)}) copy-start(f32[32,3,8,128]{3,0,2,1:T(8,128)} %get-tuple-element.247) | copy-start | bytes 1179652
  129.6 44.2 %copy-start.9 = (f32[4,8,128]{2,1,0:T(8,128)S(1)}, f32[4,8,128]{2,1,0:T(8,128)}, u32[]{:S(2)}) copy-start(f32[4,8,128]{2,1,0:T(8,128)} %param.23) | copy-start | bytes 49156
  176.3 12.1 %collective-permute-start.8 = (f32[32,4,8,1]{3,0,2,1:T(8,128)S(1)}, f32[32,4,8,1]{3,0,2,1:T(8,128)S(1)}, u32[]{:S(2)}, u32[]{:S(2)}) collective-permute-start(f32[32,4,8,1]{3,0,2,1:T(8,128)S(1)} %get-tuple-element.242), channel_id=1, source_target_pairs={{1,0},{2,1},{3,2},{4,3},{5,4},{6,5},{7,6},{9,8},{10,9},{11,10},{12... | collective-permute-start | bytes 12296 | tf_op jit(solution)/shard_map/ppermute | solution.py:23
  179.4 9.0 %collective-permute-start.9 = (f32[32,4,8,1]{3,0,2,1:T(8,128)S(1)}, f32[32,4,8,1]{3,0,2,1:T(8,128)S(1)}, u32[]{:S(2)}, u32[]{:S(2)}) collective-permute-start(f32[32,4,8,1]{3,0,2,1:T(8,128)S(1)} %get-tuple-element.243), channel_id=1, source_target_pairs={{0,1},{1,2},{2,3},{3,4},{4,5},{5,6},{6,7},{8,9},{9,10},{10,11},{11... | collective-permute-start | bytes 12296 | tf_op jit(solution)/shard_map/ppermute | solution.py:22
  181.9 6.5 collective-permute-start.6
  183.2 5.3 collective-permute-start.7
  265.4 82.0 %copy-start.16 = (f32[32,32]{0,1:T(8,128)S(1)}, f32[32,32]{0,1:T(8,128)}, u32[]{:S(2)}) copy-start(f32[32,32]{0,1:T(8,128)} %copy-done.15) | copy-start | bytes 12292
  269.8 14.1 %collective-permute-start.12 = (f32[32,4,8,1]{3,0,2,1:T(8,128)}, f32[32,4,8,1]{3,0,2,1:T(8,128)S(1)}, u32[]{:S(2)}, u32[]{:S(2)}) collective-permute-start(f32[32,4,8,1]{3,0,2,1:T(8,128)} %get-tuple-element.236), channel_id=1, source_target_pairs={{1,0},{2,1},{3,2},{4,3},{5,4},{6,5},{7,6},{9,8},{10,9},{11,10},{12... | collective-permute-start | bytes 12296 | tf_op jit(solution)/shard_map/ppermute | solution.py:23
  271.9 12.0 %collective-permute-start.13 = (f32[32,4,8,1]{3,0,2,1:T(8,128)}, f32[32,4,8,1]{3,0,2,1:T(8,128)}, u32[]{:S(2)}, u32[]{:S(2)}) collective-permute-start(f32[32,4,8,1]{3,0,2,1:T(8,128)} %get-tuple-element.237), channel_id=1, source_target_pairs={{0,1},{1,2},{2,3},{3,4},{4,5},{5,6},{6,7},{8,9},{9,10},{10,11},{11... | collective-permute-start | bytes 12296 | tf_op jit(solution)/shard_map/ppermute | solution.py:22
  275.4 8.5 %collective-permute-start.10 = (f32[32,4,1,128]{3,0,2,1:T(8,128)}, f32[32,4,1,128]{3,0,2,1:T(8,128)S(1)}, u32[]{:S(2)}, u32[]{:S(2)}) collective-permute-start(f32[32,4,1,128]{3,0,2,1:T(8,128)} %get-tuple-element.239), channel_id=1, source_target_pairs={{8,0},{16,8},{24,16},{32,24},{40,32},{48,40},{56,48},{64,56},{72,6... | collective-permute-start | bytes 196616 | tf_op jit(solution)/shard_map/ppermute | solution.py:23
  276.7 7.3 %collective-permute-start.11 = (f32[32,4,1,128]{3,0,2,1:T(8,128)}, f32[32,4,1,128]{3,0,2,1:T(8,128)S(1)}, u32[]{:S(2)}, u32[]{:S(2)}) collective-permute-start(f32[32,4,1,128]{3,0,2,1:T(8,128)} %get-tuple-element.238), channel_id=1, source_target_pairs={{0,8},{8,16},{16,24},{24,32},{32,40},{40,48},{48,56},{56,64},{64,7... | collective-permute-start | bytes 196616 | tf_op jit(solution)/shard_map/ppermute | solution.py:22
  350.4 11.6 %collective-permute-start.16 = (f32[32,4,8,1]{3,0,2,1:T(8,128)S(1)}, f32[32,4,8,1]{3,0,2,1:T(8,128)S(1)}, u32[]{:S(2)}, u32[]{:S(2)}) collective-permute-start(f32[32,4,8,1]{3,0,2,1:T(8,128)S(1)} %get-tuple-element.230), channel_id=1, source_target_pairs={{1,0},{2,1},{3,2},{4,3},{5,4},{6,5},{7,6},{9,8},{10,9},{11,10},{12... | collective-permute-start | bytes 12296 | tf_op jit(solution)/shard_map/ppermute | solution.py:23
  352.4 9.6 %collective-permute-start.17 = (f32[32,4,8,1]{3,0,2,1:T(8,128)S(1)}, f32[32,4,8,1]{3,0,2,1:T(8,128)S(1)}, u32[]{:S(2)}, u32[]{:S(2)}) collective-permute-start(f32[32,4,8,1]{3,0,2,1:T(8,128)S(1)} %get-tuple-element.231), channel_id=1, source_target_pairs={{0,1},{1,2},{2,3},{3,4},{4,5},{5,6},{6,7},{8,9},{9,10},{10,11},{11... | collective-permute-start | bytes 12296 | tf_op jit(solution)/shard_map/ppermute | solution.py:22
  355.9 6.1 collective-permute-start.14
  357.2 5.6 collective-permute-start.15
  363.9 72.2 %copy-start.17 = (f32[4,8,8,128]{3,2,1,0:T(8,128)S(1)}, f32[4,8,8,128]{3,2,1,0:T(8,128)}, u32[]{:S(2)}) copy-start(f32[4,8,8,128]{3,2,1,0:T(8,128)} %copy.319) | copy-start | bytes 393220
  424.8 11.3 %collective-permute-start.20 = (f32[32,4,8,1]{3,0,2,1:T(8,128)S(1)}, f32[32,4,8,1]{3,0,2,1:T(8,128)S(1)}, u32[]{:S(2)}, u32[]{:S(2)}) collective-permute-start(f32[32,4,8,1]{3,0,2,1:T(8,128)S(1)} %get-tuple-element.224), channel_id=1, source_target_pairs={{1,0},{2,1},{3,2},{4,3},{5,4},{6,5},{7,6},{9,8},{10,9},{11,10},{12... | collective-permute-start | bytes 12296 | tf_op jit(solution)/shard_map/ppermute | solution.py:23
  426.9 9.6 %collective-permute-start.21 = (f32[32,4,8,1]{3,0,2,1:T(8,128)S(1)}, f32[32,4,8,1]{3,0,2,1:T(8,128)S(1)}, u32[]{:S(2)}, u32[]{:S(2)}) collective-permute-start(f32[32,4,8,1]{3,0,2,1:T(8,128)S(1)} %get-tuple-element.225), channel_id=1, source_target_pairs={{0,1},{1,2},{2,3},{3,4},{4,5},{5,6},{6,7},{8,9},{9,10},{10,11},{11... | collective-permute-start | bytes 12296 | tf_op jit(solution)/shard_map/ppermute | solution.py:22
  430.4 6.1 collective-permute-start.18
  431.7 5.6 collective-permute-start.19
  438.3 11.9 %collective-permute-start.24 = (f32[32,4,8,1]{3,0,2,1:T(8,128)S(1)}, f32[32,4,8,1]{3,0,2,1:T(8,128)S(1)}, u32[]{:S(2)}, u32[]{:S(2)}) collective-permute-start(f32[32,4,8,1]{3,0,2,1:T(8,128)S(1)} %get-tuple-element.218), channel_id=1, source_target_pairs={{1,0},{2,1},{3,2},{4,3},{5,4},{6,5},{7,6},{9,8},{10,9},{11,10},{12... | collective-permute-start | bytes 12296 | tf_op jit(solution)/shard_map/ppermute | solution.py:23
  440.3 9.9 %collective-permute-start.25 = (f32[32,4,8,1]{3,0,2,1:T(8,128)S(1)}, f32[32,4,8,1]{3,0,2,1:T(8,128)S(1)}, u32[]{:S(2)}, u32[]{:S(2)}) collective-permute-start(f32[32,4,8,1]{3,0,2,1:T(8,128)S(1)} %get-tuple-element.219), channel_id=1, source_target_pairs={{0,1},{1,2},{2,3},{3,4},{4,5},{5,6},{6,7},{8,9},{9,10},{10,11},{11... | collective-permute-start | bytes 12296 | tf_op jit(solution)/shard_map/ppermute | solution.py:22
  443.8 6.3 collective-permute-start.22
  445.1 6.0 collective-permute-start.23
  528.9 82.8 %copy-start.13 = (f32[32,32]{0,1:T(8,128)S(1)}, f32[32,32]{0,1:T(8,128)}, u32[]{:S(2)}) copy-start(f32[32,32]{0,1:T(8,128)} %copy-done.12) | copy-start | bytes 12292
  533.4 14.6 %collective-permute-start.28 = (f32[32,4,8,1]{3,0,2,1:T(8,128)}, f32[32,4,8,1]{3,0,2,1:T(8,128)S(1)}, u32[]{:S(2)}, u32[]{:S(2)}) collective-permute-start(f32[32,4,8,1]{3,0,2,1:T(8,128)} %get-tuple-element.212), channel_id=1, source_target_pairs={{1,0},{2,1},{3,2},{4,3},{5,4},{6,5},{7,6},{9,8},{10,9},{11,10},{12... | collective-permute-start | bytes 12296 | tf_op jit(solution)/shard_map/ppermute | solution.py:23
  535.5 12.5 %collective-permute-start.29 = (f32[32,4,8,1]{3,0,2,1:T(8,128)}, f32[32,4,8,1]{3,0,2,1:T(8,128)}, u32[]{:S(2)}, u32[]{:S(2)}) collective-permute-start(f32[32,4,8,1]{3,0,2,1:T(8,128)} %get-tuple-element.213), channel_id=1, source_target_pairs={{0,1},{1,2},{2,3},{3,4},{4,5},{5,6},{6,7},{8,9},{9,10},{10,11},{11... | collective-permute-start | bytes 12296 | tf_op jit(solution)/shard_map/ppermute | solution.py:22
  539.0 9.0 %collective-permute-start.26 = (f32[32,4,1,128]{3,0,2,1:T(8,128)}, f32[32,4,1,128]{3,0,2,1:T(8,128)S(1)}, u32[]{:S(2)}, u32[]{:S(2)}) collective-permute-start(f32[32,4,1,128]{3,0,2,1:T(8,128)} %get-tuple-element.215), channel_id=1, source_target_pairs={{8,0},{16,8},{24,16},{32,24},{40,32},{48,40},{56,48},{64,56},{72,6... | collective-permute-start | bytes 196616 | tf_op jit(solution)/shard_map/ppermute | solution.py:23
  540.3 7.7 %collective-permute-start.27 = (f32[32,4,1,128]{3,0,2,1:T(8,128)}, f32[32,4,1,128]{3,0,2,1:T(8,128)S(1)}, u32[]{:S(2)}, u32[]{:S(2)}) collective-permute-start(f32[32,4,1,128]{3,0,2,1:T(8,128)} %get-tuple-element.214), channel_id=1, source_target_pairs={{0,8},{8,16},{16,24},{24,32},{32,40},{40,48},{48,56},{56,64},{64,7... | collective-permute-start | bytes 196616 | tf_op jit(solution)/shard_map/ppermute | solution.py:22
  550.6 62.6 %copy-start.14 = (f32[32,32]{0,1:T(8,128)S(1)}, f32[32,32]{0,1:T(8,128)}, u32[]{:S(2)}) copy-start(f32[32,32]{0,1:T(8,128)} %copy-done.12) | copy-start | bytes 12292
  550.6 62.8 %copy-start.21 = (f32[1,32,32]{1,2,0:T(8,128)S(1)}, f32[1,32,32]{1,2,0:T(8,128)}, u32[]{:S(2)}) copy-start(f32[1,32,32]{1,2,0:T(8,128)} %custom-call.25) | copy-start | bytes 12292
  614.6 11.6 %collective-permute-start.32 = (f32[32,4,8,1]{3,0,2,1:T(8,128)S(1)}, f32[32,4,8,1]{3,0,2,1:T(8,128)S(1)}, u32[]{:S(2)}, u32[]{:S(2)}) collective-permute-start(f32[32,4,8,1]{3,0,2,1:T(8,128)S(1)} %get-tuple-element.206), channel_id=1, source_target_pairs={{1,0},{2,1},{3,2},{4,3},{5,4},{6,5},{7,6},{9,8},{10,9},{11,10},{12... | collective-permute-start | bytes 12296 | tf_op jit(solution)/shard_map/ppermute | solution.py:23
  616.7 9.6 %collective-permute-start.33 = (f32[32,4,8,1]{3,0,2,1:T(8,128)S(1)}, f32[32,4,8,1]{3,0,2,1:T(8,128)S(1)}, u32[]{:S(2)}, u32[]{:S(2)}) collective-permute-start(f32[32,4,8,1]{3,0,2,1:T(8,128)S(1)} %get-tuple-element.207), channel_id=1, source_target_pairs={{0,1},{1,2},{2,3},{3,4},{4,5},{5,6},{6,7},{8,9},{9,10},{10,11},{11... | collective-permute-start | bytes 12296 | tf_op jit(solution)/shard_map/ppermute | solution.py:22
  620.2 6.1 collective-permute-start.30
  621.5 5.6 collective-permute-start.31
  (17 other events, 172.8 us)
where the time goes:
time: 702 us; the launch traced here: 691 us
  blocking collectives  321 us (46%)
  starting transfers between devices  117 us (17%)
  other arithmetic  87.7 us (12%)
  local copies, waits for them, and re-layouts  82.2 us (12%)
  matrix products  69.4 us (10%)
  waiting for transfers between devices  11.7 us (2%)
    psum x24, blocking collectives, by_axis(): return functools.reduce(lax.psum, axes, x)  321 us
    ppermute x16, starting transfers between devices, with_halo(): lax.ppermute(last, axis, up)  59.3 us
    dot_general x16, matrix products, add_block(): jnp.dot(piece_values, one_hot, preferred_element_type=jnp.float32)  43 us
    unnamed x63, local copies, waits for them, and re-layouts  38.7 us
    another operation x30, other arithmetic, spd_solve(): factor = jnp.linalg.cholesky(matrix)  35.9 us
    another operation x20, other arithmetic, spd_solve(): return jax.scipy.linalg.cho_solve((factor, True), right)  31.4 us
    ppermute x16, starting transfers between devices, with_halo(): lax.ppermute(initial, axis, [(b, a) for a, b in up])  27.8 us
    scatter x1, local copies, waits for them, and re-layouts, body(): jnp.zeros((currents.shape[0], slots_all), jnp.bfloat16).at[:, slot_index]  23.6 us
  transfers between devices with their start and end apart: 36, of which 9 were waited for; matrix products, arithmetic and copies ran while one was open for 14% of the time, Pallas kernels for 0%

commit v1 on v0

--- a/solution.py
+++ b/solution.py
@@ -9,6 +9,15 @@
 GX_GY = ("gx_0", "gx_1", "gy_0", "gy_1")
 GX = ("gx_0", "gx_1")
 GY = ("gy_0", "gy_1")
+threads_recast = lambda row_data, axis_name: jnp.concatenate(
+    lax.all_to_all(
+        jnp.stack(jnp.split(row_data, lax.axis_size(axis_name), 1), 0),
+        split_axis=0,
+        concat_axis=0,
+        axis_name=axis_name,
+    ),
+    1,
+)
 
 
 def with_halo(x, sides, width):
@@ -101,7 +110,7 @@
     cell_slots = jnp.zeros((1, slots_all), jnp.int32).at[0, slot_index].set(cells)
     arrived, cell_slots = (
         lax.all_to_all(packed, GX_GY, split_axis=1, concat_axis=1, tiled=True),
-        lax.all_to_all(cell_slots, GX_GY, split_axis=1, concat_axis=1, tiled=True),
+        threads_recast(cell_slots, GX_GY),
     )
     block_rows = min(1024, slots_all)
     block_count = slots_all // block_rows

time: 702 us -> 771 us (1.098)
  local copies, waits for them, and re-layouts: 82.2 us -> 151 us
    unnamed x63 -> x190, local copies, waits for them, and re-layouts: 38.7 us -> 107 us
  transfers between devices with their start and end apart: 36 -> 36, of which waited for: 9 -> 9; matrix products, arithmetic and copies ran while one was open for 14% -> 21% of each run, Pallas kernels for 0% -> 0%
where the time goes in v1:
time: 771 us; the launch traced here: 761 us
  blocking collectives  321 us (42%)
  local copies, waits for them, and re-layouts  151 us (20%)
  starting transfers between devices  117 us (15%)
  other arithmetic  87.7 us (11%)
  matrix products  69.4 us (9%)
  waiting for transfers between devices  11.7 us (2%)
    psum x24, blocking collectives, by_axis(): return functools.reduce(lax.psum, axes, x)  321 us
    unnamed x190, local copies, waits for them, and re-layouts  107 us
    ppermute x16, starting transfers between devices, with_halo(): lax.ppermute(last, axis, up)  59.2 us
    dot_general x16, matrix products, add_block(): jnp.dot(piece_values, one_hot, preferred_element_type=jnp.float32)  43 us
    another operation x30, other arithmetic, spd_solve(): factor = jnp.linalg.cholesky(matrix)  35.9 us
    another operation x20, other arithmetic, spd_solve(): return jax.scipy.linalg.cho_solve((factor, True), right)  31.4 us
    ppermute x16, starting transfers between devices, with_halo(): lax.ppermute(initial, axis, [(b, a) for a, b in up])  28 us
    scatter x1, local copies, waits for them, and re-layouts, body(): jnp.zeros((currents.shape[0], slots_all), jnp.bfloat16).at[:, slot_index]  23.6 us
  transfers between devices with their start and end apart: 36, of which 9 were waited for; matrix products, arithmetic and copies ran while one was open for 21% of the time, Pallas kernels for 0%

profile of v1, /device:TPU:1, one launch (start us, length us, event | category | flops | bytes accessed | tf_op | source)
XLA Modules:
  0.0 760.7 jit_solution(7004924391856724217)
XLA Ops:
  4.7 5.3 select_reduce_fusion
  12.3 23.6 %scatter_custom_fusion = bf16[64,16384]{0,1:T(8,128)(2,1)} fusion(s32[8192]{0:T(1024)S(1)} %bitcast.854, bf16[8192,64]{1,0:T(8,128)(2,1)S(1)} %copy.198, bf16[]{:T(256)} %constant.128.clone.1), kind=kCustom, calls=%fused_computation.18 | custom fusion | bytes 2097154 | tf_op jit(solution)/shard_map/scatter | solution.py:109
  36.0 4.8 copy.199
  40.8 11.5 %all-to-all-start = ((bf16[64,128,128]{2,0,1:T(8,128)(2,1)}), bf16[64,128,128]{2,0,1:T(8,128)(2,1)S(1)}, u32[]{:S(2)}, u32[]{:S(2)}) async-start(bf16[64,128,128]{2,0,1:T(8,128)(2,1)} %copy.199), calls=%async_computation | async-start | bytes 4194304 | tf_op jit(solution)/shard_map/all_to_all | solution.py:112
  58.6 3.8 collective-permute-start.4
  62.4 4.3 collective-permute-start.1
  70.1 30.7 %scatter_custom_fusion.1 = s32[16384]{0:T(1024)S(1)} fusion(s32[8192]{0:T(1024)S(1)} %broadcast_select_fusion, s32[8192]{0:T(1024)} %param.26, s32[]{:T(128)} %constant.126.clone.1), kind=kCustom, calls=%fused_computation.418 | custom fusion | bytes 66048
  171.5 3.8 collective-permute-start.5
  178.7 10.5 %all-to-all-start.1 = ((s32[128,1,128]{2,1,0:T(1,128)}), s32[128,1,128]{2,1,0:T(1,128)S(1)}, u32[]{:S(2)}, u32[]{:S(2)}) async-start(s32[128,1,128]{2,1,0:T(1,128)} %constant_dynamic-update-slice_fusion), calls=%async_computation.1 | async-start | bytes 131072 | tf_op jit(solution)/shard_map/all_to_all | solution.py:13
  190.8 7.7 %all-to-all-done.1 = s32[128,1,128]{2,1,0:T(1,128)S(1)} async-done(((s32[128,1,128]{2,1,0:T(1,128)}), s32[128,1,128]{2,1,0:T(1,128)S(1)}, u32[]{:S(2)}, u32[]{:S(2)}) %all-to-all-start.1) | async-done | bytes 65568 | tf_op jit(solution)/shard_map/all_to_all | solution.py:13
  198.6 43.1 %while.16 = (s32[]{:T(128)}, f32[64,1024]{1,0:T(8,128)}, bf16[64,16384]{1,0:T(8,128)(2,1)}, s32[128,1,128]{2,1,0:T(1,128)S(1)}, s32[]{:T(128)}, /*index=5*/s32[]{:T(128)}, s32[]{:T(128)}, s32[]{:T(128)}) while((s32[]{:T(128)}, f32[64,1024]{1,0:T(8,128)}, bf16[64,16384]{1,0:T(8,128)(2,1)}, s32[128,1,128]{2,1,0:T(1,128)S(1)}, ...), condition=%wide.region_6.7_spmd.clone, body=%wide.region_5.6_spmd.clone.sunk | while | flops 135397376 | bytes 667797 | solution.py:125
  252.2 4.0 collective-permute-start.7
  259.3 16.8 %all-reduce.45 = (f32[32,32]{0,1:T(8,128)S(1)}, f32[32,32]{0,1:T(8,128)S(1)}, f32[32,32]{1,0:T(8,128)S(1)}) all-reduce(f32[32,32]{0,1:T(8,128)S(1)} %convolution_bitcast_fusion.18, f32[32,32]{0,1:T(8,128)S(1)} %convolution_bitcast_fusion.19, ...), channel_id=1, replica_groups=mesh['gx_0'=4,'gx_1'=4,'gy_0'=4,'gy_1'=2] {'gx_0'}, use_global_device_ids=true, to_apply=%region_13.15 | all-reduce | flops 3072 | bytes 24576 | tf_op jit(solution)/shard_map/psum | solution.py:50
  276.1 11.2 %all-reduce.41 = (f32[32,32]{0,1:T(8,128)S(1)}, f32[32,32]{0,1:T(8,128)S(1)}, f32[32,32]{1,0:T(8,128)S(1)}) all-reduce(f32[32,32]{0,1:T(8,128)S(1)} %get-tuple-element.189, f32[32,32]{0,1:T(8,128)S(1)} %get-tuple-element.190, f32[32,32]{1,0:T(8,128)S(1)} %get-tuple-element.191), channel_id=1, replica_groups=mesh['gx_0'=4,'gx_1'=4,'gy_0'=4,'gy_1'=2] {'gx_1'}, use_global_device_ids=true, to_apply=%region_14.16 | all-reduce | flops 3072 | bytes 24576 | tf_op jit(solution)/shard_map/psum | solution.py:50
  287.3 11.7 %all-reduce.37 = (f32[32,32]{0,1:T(8,128)S(1)}, f32[32,32]{0,1:T(8,128)S(1)}, f32[32,32]{1,0:T(8,128)S(1)}) all-reduce(f32[32,32]{0,1:T(8,128)S(1)} %get-tuple-element.177, f32[32,32]{0,1:T(8,128)S(1)} %get-tuple-element.178, f32[32,32]{1,0:T(8,128)S(1)} %get-tuple-element.179), channel_id=1, replica_groups=mesh['gx_0'=4,'gx_1'=4,'gy_0'=4,'gy_1'=2] {'gy_0'}, use_global_device_ids=true, to_apply=%region_15.17 | all-reduce | flops 3072 | bytes 24576 | tf_op jit(solution)/shard_map/psum | solution.py:50
  299.0 15.0 %all-reduce.49 = (f32[32,32]{0,1:T(8,128)S(1)}, f32[32,32]{0,1:T(8,128)S(1)}, f32[32,32]{1,0:T(8,128)S(1)}) all-reduce(f32[32,32]{0,1:T(8,128)S(1)} %get-tuple-element.165, f32[32,32]{0,1:T(8,128)S(1)} %get-tuple-element.166, f32[32,32]{1,0:T(8,128)S(1)} %get-tuple-element.167), channel_id=1, replica_groups=mesh['gx_0'=4,'gx_1'=4,'gy_0'=4,'gy_1'=2] {'gy_1'}, use_global_device_ids=true, to_apply=%region_16.18 | all-reduce | flops 3072 | bytes 24576 | tf_op jit(solution)/shard_map/psum | solution.py:50
  340.9 3.5 collective-permute-start.13
  345.9 4.0 collective-permute-start.11
  357.2 14.7 %all-reduce.44 = (f32[32,32]{0,1:T(8,128)S(1)}, f32[32,32]{1,0:T(8,128)S(1)}, f32[32,32]{1,0:T(8,128)S(1)}) all-reduce(f32[32,32]{0,1:T(8,128)S(1)} %convolution_bitcast_fusion.15, f32[32,32]{1,0:T(8,128)S(1)} %convolution_bitcast_fusion.13, ...), channel_id=1, replica_groups=mesh['gx_0'=4,'gx_1'=4,'gy_0'=4,'gy_1'=2] {'gx_0'}, use_global_device_ids=true, to_apply=%region_21.24 | all-reduce | flops 3072 | bytes 24576 | tf_op jit(solution)/shard_map/psum | solution.py:50
  372.0 11.4 %all-reduce.40 = (f32[32,32]{0,1:T(8,128)S(1)}, f32[32,32]{1,0:T(8,128)S(1)}, f32[32,32]{1,0:T(8,128)S(1)}) all-reduce(f32[32,32]{0,1:T(8,128)S(1)} %get-tuple-element.186, f32[32,32]{1,0:T(8,128)S(1)} %get-tuple-element.187, f32[32,32]{1,0:T(8,128)S(1)} %get-tuple-element.188), channel_id=1, replica_groups=mesh['gx_0'=4,'gx_1'=4,'gy_0'=4,'gy_1'=2] {'gx_1'}, use_global_device_ids=true, to_apply=%region_22.25 | all-reduce | flops 3072 | bytes 24576 | tf_op jit(solution)/shard_map/psum | solution.py:50
  383.4 11.2 %all-reduce.36 = (f32[32,32]{0,1:T(8,128)S(1)}, f32[32,32]{1,0:T(8,128)S(1)}, f32[32,32]{1,0:T(8,128)S(1)}) all-reduce(f32[32,32]{0,1:T(8,128)S(1)} %get-tuple-element.174, f32[32,32]{1,0:T(8,128)S(1)} %get-tuple-element.175, f32[32,32]{1,0:T(8,128)S(1)} %get-tuple-element.176), channel_id=1, replica_groups=mesh['gx_0'=4,'gx_1'=4,'gy_0'=4,'gy_1'=2] {'gy_0'}, use_global_device_ids=true, to_apply=%region_23.26 | all-reduce | flops 3072 | bytes 24576 | tf_op jit(solution)/shard_map/psum | solution.py:50
  394.6 15.1 %all-reduce.48 = (f32[32,32]{0,1:T(8,128)S(1)}, f32[32,32]{1,0:T(8,128)S(1)}, f32[32,32]{1,0:T(8,128)S(1)}) all-reduce(f32[32,32]{0,1:T(8,128)S(1)} %get-tuple-element.162, f32[32,32]{1,0:T(8,128)S(1)} %get-tuple-element.163, f32[32,32]{1,0:T(8,128)S(1)} %get-tuple-element.164), channel_id=1, replica_groups=mesh['gx_0'=4,'gx_1'=4,'gy_0'=4,'gy_1'=2] {'gy_1'}, use_global_device_ids=true, to_apply=%region_24.27 | all-reduce | flops 3072 | bytes 24576 | tf_op jit(solution)/shard_map/psum | solution.py:50
  421.5 3.5 collective-permute-start.17
  426.2 4.0 collective-permute-start.15
  432.9 16.2 %psum.440 = f32[32,32]{0,1:T(8,128)S(1)} all-reduce(f32[32,32]{0,1:T(8,128)S(1)} %convolution_bitcast_fusion.11), channel_id=1, replica_groups=mesh['gx_0'=4,'gx_1'=4,'gy_0'=4,'gy_1'=2] {'gx_0'}, use_global_device_ids=true, to_apply=%region_33.36 | all-reduce | flops 1024 | bytes 8192 | tf_op jit(solution)/shard_map/psum | solution.py:50
  449.1 10.8 %psum.441 = f32[32,32]{0,1:T(8,128)S(1)} all-reduce(f32[32,32]{0,1:T(8,128)S(1)} %psum.440), channel_id=1, replica_groups=mesh['gx_0'=4,'gx_1'=4,'gy_0'=4,'gy_1'=2] {'gx_1'}, use_global_device_ids=true, to_apply=%region_34.37 | all-reduce | flops 1024 | bytes 8192 | tf_op jit(solution)/shard_map/psum | solution.py:50
  459.9 10.8 %psum.442 = f32[32,32]{0,1:T(8,128)S(1)} all-reduce(f32[32,32]{0,1:T(8,128)S(1)} %psum.441), channel_id=1, replica_groups=mesh['gx_0'=4,'gx_1'=4,'gy_0'=4,'gy_1'=2] {'gy_0'}, use_global_device_ids=true, to_apply=%region_35.38 | all-reduce | flops 1024 | bytes 8192 | tf_op jit(solution)/shard_map/psum | solution.py:50
  470.7 15.2 %psum.443 = f32[32,32]{0,1:T(8,128)S(1)} all-reduce(f32[32,32]{0,1:T(8,128)S(1)} %psum.442), channel_id=1, replica_groups=mesh['gx_0'=4,'gx_1'=4,'gy_0'=4,'gy_1'=2] {'gy_1'}, use_global_device_ids=true, to_apply=%region_36.39 | all-reduce | flops 1024 | bytes 8192 | tf_op jit(solution)/shard_map/psum | solution.py:50
  496.1 3.5 collective-permute-start.21
  500.9 4.4 collective-permute-start.19
  509.5 3.6 collective-permute-start.25
  514.4 4.4 collective-permute-start.23
  522.2 18.0 %all-reduce.43 = (f32[32,32]{0,1:T(8,128)S(1)}, f32[32,32]{0,1:T(8,128)S(1)}, f32[32,32]{1,0:T(8,128)S(1)}) all-reduce(f32[32,32]{0,1:T(8,128)S(1)} %convolution_bitcast_fusion.8, f32[32,32]{0,1:T(8,128)S(1)} %convolution_bitcast_fusion.9, ...), channel_id=1, replica_groups=mesh['gx_0'=4,'gx_1'=4,'gy_0'=4,'gy_1'=2] {'gx_0'}, use_global_device_ids=true, to_apply=%region_41.44 | all-reduce | flops 3072 | bytes 24576 | tf_op jit(solution)/shard_map/psum | solution.py:50
  540.2 11.2 %all-reduce.39 = (f32[32,32]{0,1:T(8,128)S(1)}, f32[32,32]{0,1:T(8,128)S(1)}, f32[32,32]{1,0:T(8,128)S(1)}) all-reduce(f32[32,32]{0,1:T(8,128)S(1)} %get-tuple-element.183, f32[32,32]{0,1:T(8,128)S(1)} %get-tuple-element.184, f32[32,32]{1,0:T(8,128)S(1)} %get-tuple-element.185), channel_id=1, replica_groups=mesh['gx_0'=4,'gx_1'=4,'gy_0'=4,'gy_1'=2] {'gx_1'}, use_global_device_ids=true, to_apply=%region_42.45 | all-reduce | flops 3072 | bytes 24576 | tf_op jit(solution)/shard_map/psum | solution.py:50
  551.5 11.2 %all-reduce.35 = (f32[32,32]{0,1:T(8,128)S(1)}, f32[32,32]{0,1:T(8,128)S(1)}, f32[32,32]{1,0:T(8,128)S(1)}) all-reduce(f32[32,32]{0,1:T(8,128)S(1)} %get-tuple-element.171, f32[32,32]{0,1:T(8,128)S(1)} %get-tuple-element.172, f32[32,32]{1,0:T(8,128)S(1)} %get-tuple-element.173), channel_id=1, replica_groups=mesh['gx_0'=4,'gx_1'=4,'gy_0'=4,'gy_1'=2] {'gy_0'}, use_global_device_ids=true, to_apply=%region_43.46 | all-reduce | flops 3072 | bytes 24576 | tf_op jit(solution)/shard_map/psum | solution.py:50
  562.7 15.2 %all-reduce.47 = (f32[32,32]{0,1:T(8,128)S(1)}, f32[32,32]{0,1:T(8,128)S(1)}, f32[32,32]{1,0:T(8,128)S(1)}) all-reduce(f32[32,32]{0,1:T(8,128)S(1)} %get-tuple-element.159, f32[32,32]{0,1:T(8,128)S(1)} %get-tuple-element.160, f32[32,32]{1,0:T(8,128)S(1)} %get-tuple-element.161), channel_id=1, replica_groups=mesh['gx_0'=4,'gx_1'=4,'gy_0'=4,'gy_1'=2] {'gy_1'}, use_global_device_ids=true, to_apply=%region_44.47 | all-reduce | flops 3072 | bytes 24576 | tf_op jit(solution)/shard_map/psum | solution.py:50
  604.7 3.5 collective-permute-start.29
  609.5 4.0 collective-permute-start.27
  621.5 14.3 %all-reduce.42 = (f32[32,32]{0,1:T(8,128)S(1)}, f32[32,32]{1,0:T(8,128)S(1)}, f32[32,32]{1,0:T(8,128)S(1)}) all-reduce(f32[32,32]{0,1:T(8,128)S(1)} %convolution_bitcast_fusion.5, f32[32,32]{1,0:T(8,128)S(1)} %convolution_bitcast_fusion.3, ...), channel_id=1, replica_groups=mesh['gx_0'=4,'gx_1'=4,'gy_0'=4,'gy_1'=2] {'gx_0'}, use_global_device_ids=true, to_apply=%region_49.52 | all-reduce | flops 3072 | bytes 24576 | tf_op jit(solution)/shard_map/psum | solution.py:50
  635.8 12.1 %all-reduce.38 = (f32[32,32]{0,1:T(8,128)S(1)}, f32[32,32]{1,0:T(8,128)S(1)}, f32[32,32]{1,0:T(8,128)S(1)}) all-reduce(f32[32,32]{0,1:T(8,128)S(1)} %get-tuple-element.180, f32[32,32]{1,0:T(8,128)S(1)} %get-tuple-element.181, f32[32,32]{1,0:T(8,128)S(1)} %get-tuple-element.182), channel_id=1, replica_groups=mesh['gx_0'=4,'gx_1'=4,'gy_0'=4,'gy_1'=2] {'gx_1'}, use_global_device_ids=true, to_apply=%region_50.53 | all-reduce | flops 3072 | bytes 24576 | tf_op jit(solution)/shard_map/psum | solution.py:50
  647.9 11.2 %all-reduce.34 = (f32[32,32]{0,1:T(8,128)S(1)}, f32[32,32]{1,0:T(8,128)S(1)}, f32[32,32]{1,0:T(8,128)S(1)}) all-reduce(f32[32,32]{0,1:T(8,128)S(1)} %get-tuple-element.168, f32[32,32]{1,0:T(8,128)S(1)} %get-tuple-element.169, f32[32,32]{1,0:T(8,128)S(1)} %get-tuple-element.170), channel_id=1, replica_groups=mesh['gx_0'=4,'gx_1'=4,'gy_0'=4,'gy_1'=2] {'gy_0'}, use_global_device_ids=true, to_apply=%region_51.54 | all-reduce | flops 3072 | bytes 24576 | tf_op jit(solution)/shard_map/psum | solution.py:50
  659.2 15.0 %all-reduce.46 = (f32[32,32]{0,1:T(8,128)S(1)}, f32[32,32]{1,0:T(8,128)S(1)}, f32[32,32]{1,0:T(8,128)S(1)}) all-reduce(f32[32,32]{0,1:T(8,128)S(1)} %get-tuple-element.156, f32[32,32]{1,0:T(8,128)S(1)} %get-tuple-element.157, f32[32,32]{1,0:T(8,128)S(1)} %get-tuple-element.158), channel_id=1, replica_groups=mesh['gx_0'=4,'gx_1'=4,'gy_0'=4,'gy_1'=2] {'gy_1'}, use_global_device_ids=true, to_apply=%region_52.55 | all-reduce | flops 3072 | bytes 24576 | tf_op jit(solution)/shard_map/psum | solution.py:50
  686.0 3.5 collective-permute-start.33
  690.7 4.0 collective-permute-start.31
  697.6 15.4 %psum.468 = f32[32,32]{0,1:T(8,128)S(1)} all-reduce(f32[32,32]{0,1:T(8,128)S(1)} %convolution_bitcast_fusion.1), channel_id=1, replica_groups=mesh['gx_0'=4,'gx_1'=4,'gy_0'=4,'gy_1'=2] {'gx_0'}, use_global_device_ids=true, to_apply=%region_61.64 | all-reduce | flops 1024 | bytes 8192 | tf_op jit(solution)/shard_map/psum | solution.py:50
  713.0 10.8 %psum.469 = f32[32,32]{0,1:T(8,128)S(1)} all-reduce(f32[32,32]{0,1:T(8,128)S(1)} %psum.468), channel_id=1, replica_groups=mesh['gx_0'=4,'gx_1'=4,'gy_0'=4,'gy_1'=2] {'gx_1'}, use_global_device_ids=true, to_apply=%region_62.65 | all-reduce | flops 1024 | bytes 8192 | tf_op jit(solution)/shard_map/psum | solution.py:50
  723.8 10.8 %psum.470 = f32[32,32]{0,1:T(8,128)S(1)} all-reduce(f32[32,32]{0,1:T(8,128)S(1)} %psum.469), channel_id=1, replica_groups=mesh['gx_0'=4,'gx_1'=4,'gy_0'=4,'gy_1'=2] {'gy_0'}, use_global_device_ids=true, to_apply=%region_63.66 | all-reduce | flops 1024 | bytes 8192 | tf_op jit(solution)/shard_map/psum | solution.py:50
  734.6 15.2 %psum.471 = f32[32,32]{0,1:T(8,128)S(1)} all-reduce(f32[32,32]{0,1:T(8,128)S(1)} %psum.470), channel_id=1, replica_groups=mesh['gx_0'=4,'gx_1'=4,'gy_0'=4,'gy_1'=2] {'gy_1'}, use_global_device_ids=true, to_apply=%region_64.67 | all-reduce | flops 1024 | bytes 8192 | tf_op jit(solution)/shard_map/psum | solution.py:50
  (466 shorter events, 281.7 us)
Async XLA Ops:
  40.8 29.1 %copy-start.25 = (s32[2]{0:T(128)S(1)}, s32[2]{0:T(128)}, u32[]{:S(2)}) copy-start(s32[2]{0:T(128)} %constant.208) | copy-start | bytes 28
  40.8 130.6 %slice-start = ((f32[4,8,128]{2,1,0:T(8,128)}), f32[3,8,128]{2,1,0:T(8,128)S(1)}, s32[]{:S(2)}) async-start(f32[4,8,128]{2,1,0:T(8,128)} %param.23), calls=%async_computation.2 | async-start | bytes 24576 | tf_op jit(solution)/shard_map/slice | solution.py:133
  40.8 135.9 %copy-start.6 = (f32[4,8,128]{2,1,0:T(8,128)S(1)}, f32[4,8,128]{2,1,0:T(8,128)}, u32[]{:S(2)}) copy-start(f32[4,8,128]{2,1,0:T(8,128)} %param.20) | copy-start | bytes 49156
  40.8 137.9 %all-to-all-start = ((bf16[64,128,128]{2,0,1:T(8,128)(2,1)}), bf16[64,128,128]{2,0,1:T(8,128)(2,1)S(1)}, u32[]{:S(2)}, u32[]{:S(2)}) async-start(bf16[64,128,128]{2,0,1:T(8,128)(2,1)} %copy.199), calls=%async_computation | async-start | bytes 4194304 | tf_op jit(solution)/shard_map/all_to_all | solution.py:112
  53.3 122.8 %collective-permute-start.2 = (f32[32,4,1,128]{3,0,2,1:T(8,128)}, f32[32,4,1,128]{3,0,2,1:T(8,128)S(1)}, u32[]{:S(2)}, u32[]{:S(2)}) collective-permute-start(f32[32,4,1,128]{3,0,2,1:T(8,128)} %get-tuple-element.251), channel_id=1, source_target_pairs={{0,8},{8,16},{16,24},{24,32},{32,40},{40,48},{48,56},{56,64},{64,7... | collective-permute-start | bytes 196616 | tf_op jit(solution)/shard_map/ppermute | solution.py:31
  56.6 121.4 %collective-permute-start = (f32[32,4,1,128]{3,0,2,1:T(8,128)S(1)}, f32[32,4,1,128]{3,0,2,1:T(8,128)S(1)}, u32[]{:S(2)}, u32[]{:S(2)}) collective-permute-start(f32[32,4,1,128]{3,0,2,1:T(8,128)S(1)} %get-tuple-element.250), channel_id=1, source_target_pairs={{8,0},{16,8},{24,16},{32,24},{40,32},{48,40},{56,48},{64,56},{72,6... | collective-permute-start | bytes 196616 | tf_op jit(solution)/shard_map/ppermute | solution.py:32
  58.6 112.9 %collective-permute-start.4 = (f32[4,8,1]{2,1,0:T(8,128)}, f32[4,8,1]{2,1,0:T(8,128)}, u32[]{:S(2)}, u32[]{:S(2)}) collective-permute-start(f32[4,8,1]{2,1,0:T(8,128)} %slice.379), channel_id=1, source_target_pairs={{0,1},{1,2},{2,3},{3,4},{4,5},{5,6},{6,7},{8,9},{9,10},{10,11},{11... | collective-permute-start | bytes 392 | tf_op jit(solution)/shard_map/ppermute | solution.py:46
  62.4 113.7 %collective-permute-start.1 = (f32[4,1,128]{2,1,0:T(1,128)S(1)}, f32[4,1,128]{2,1,0:T(1,128)S(1)}, u32[]{:S(2)}, u32[]{:S(2)}) collective-permute-start(f32[4,1,128]{2,1,0:T(1,128)S(1)} %slice.373), channel_id=1, source_target_pairs={{0,8},{8,16},{16,24},{24,32},{32,40},{40,48},{48,56},{56,64},{64,7... | collective-permute-start | bytes 6152 | tf_op jit(solution)/shard_map/ppermute | solution.py:46
  67.8 174.9 %collective-permute-start.3 = (f32[32,4,8,1]{3,0,2,1:T(8,128)}, f32[32,4,8,1]{3,0,2,1:T(8,128)}, u32[]{:S(2)}, u32[]{:S(2)}) collective-permute-start(f32[32,4,8,1]{3,0,2,1:T(8,128)} %get-tuple-element.248), channel_id=1, source_target_pairs={{1,0},{2,1},{3,2},{4,3},{5,4},{6,5},{7,6},{9,8},{10,9},{11,10},{12... | collective-permute-start | bytes 12296 | tf_op jit(solution)/shard_map/ppermute | solution.py:32
  171.5 71.3 %collective-permute-start.5 = (f32[32,4,8,1]{3,0,2,1:T(8,128)}, f32[32,4,8,1]{3,0,2,1:T(8,128)}, u32[]{:S(2)}, u32[]{:S(2)}) collective-permute-start(f32[32,4,8,1]{3,0,2,1:T(8,128)} %get-tuple-element.249), channel_id=1, source_target_pairs={{0,1},{1,2},{2,3},{3,4},{4,5},{5,6},{6,7},{8,9},{9,10},{10,11},{11... | collective-permute-start | bytes 12296 | tf_op jit(solution)/shard_map/ppermute | solution.py:31
  178.7 19.9 %all-to-all-start.1 = ((s32[128,1,128]{2,1,0:T(1,128)}), s32[128,1,128]{2,1,0:T(1,128)S(1)}, u32[]{:S(2)}, u32[]{:S(2)}) async-start(s32[128,1,128]{2,1,0:T(1,128)} %constant_dynamic-update-slice_fusion), calls=%async_computation.1 | async-start | bytes 131072 | tf_op jit(solution)/shard_map/all_to_all | solution.py:13
  198.6 44.1 %copy-start.3 = (f32[32,4,8,128]{3,0,2,1:T(8,128)S(1)}, f32[32,4,8,128]{3,0,2,1:T(8,128)}, u32[]{:S(2)}) copy-start(f32[32,4,8,128]{3,0,2,1:T(8,128)} %get-tuple-element.253) | copy-start | bytes 1572868
  198.6 44.2 %copy-start.4 = (f32[32,3,8,128]{3,0,2,1:T(8,128)S(1)}, f32[32,3,8,128]{3,0,2,1:T(8,128)}, u32[]{:S(2)}) copy-start(f32[32,3,8,128]{3,0,2,1:T(8,128)} %get-tuple-element.246) | copy-start | bytes 1179652
  198.6 44.2 %copy-start.5 = (f32[32,3,8,128]{3,0,2,1:T(8,128)S(1)}, f32[32,3,8,128]{3,0,2,1:T(8,128)}, u32[]{:S(2)}) copy-start(f32[32,3,8,128]{3,0,2,1:T(8,128)} %get-tuple-element.247) | copy-start | bytes 1179652
  198.6 44.2 %copy-start.9 = (f32[4,8,128]{2,1,0:T(8,128)S(1)}, f32[4,8,128]{2,1,0:T(8,128)}, u32[]{:S(2)}) copy-start(f32[4,8,128]{2,1,0:T(8,128)} %param.23) | copy-start | bytes 49156
  245.3 12.1 %collective-permute-start.8 = (f32[32,4,8,1]{3,0,2,1:T(8,128)S(1)}, f32[32,4,8,1]{3,0,2,1:T(8,128)S(1)}, u32[]{:S(2)}, u32[]{:S(2)}) collective-permute-start(f32[32,4,8,1]{3,0,2,1:T(8,128)S(1)} %get-tuple-element.242), channel_id=1, source_target_pairs={{1,0},{2,1},{3,2},{4,3},{5,4},{6,5},{7,6},{9,8},{10,9},{11,10},{12... | collective-permute-start | bytes 12296 | tf_op jit(solution)/shard_map/ppermute | solution.py:32
  248.4 9.0 %collective-permute-start.9 = (f32[32,4,8,1]{3,0,2,1:T(8,128)S(1)}, f32[32,4,8,1]{3,0,2,1:T(8,128)S(1)}, u32[]{:S(2)}, u32[]{:S(2)}) collective-permute-start(f32[32,4,8,1]{3,0,2,1:T(8,128)S(1)} %get-tuple-element.243), channel_id=1, source_target_pairs={{0,1},{1,2},{2,3},{3,4},{4,5},{5,6},{6,7},{8,9},{9,10},{10,11},{11... | collective-permute-start | bytes 12296 | tf_op jit(solution)/shard_map/ppermute | solution.py:31
  250.9 6.5 collective-permute-start.6
  252.2 5.3 collective-permute-start.7
  334.4 82.1 %copy-start.16 = (f32[32,32]{0,1:T(8,128)S(1)}, f32[32,32]{0,1:T(8,128)}, u32[]{:S(2)}) copy-start(f32[32,32]{0,1:T(8,128)} %copy-done.15) | copy-start | bytes 12292
  338.8 14.1 %collective-permute-start.12 = (f32[32,4,8,1]{3,0,2,1:T(8,128)}, f32[32,4,8,1]{3,0,2,1:T(8,128)S(1)}, u32[]{:S(2)}, u32[]{:S(2)}) collective-permute-start(f32[32,4,8,1]{3,0,2,1:T(8,128)} %get-tuple-element.236), channel_id=1, source_target_pairs={{1,0},{2,1},{3,2},{4,3},{5,4},{6,5},{7,6},{9,8},{10,9},{11,10},{12... | collective-permute-start | bytes 12296 | tf_op jit(solution)/shard_map/ppermute | solution.py:32
  340.9 12.0 %collective-permute-start.13 = (f32[32,4,8,1]{3,0,2,1:T(8,128)}, f32[32,4,8,1]{3,0,2,1:T(8,128)}, u32[]{:S(2)}, u32[]{:S(2)}) collective-permute-start(f32[32,4,8,1]{3,0,2,1:T(8,128)} %get-tuple-element.237), channel_id=1, source_target_pairs={{0,1},{1,2},{2,3},{3,4},{4,5},{5,6},{6,7},{8,9},{9,10},{10,11},{11... | collective-permute-start | bytes 12296 | tf_op jit(solution)/shard_map/ppermute | solution.py:31
  344.4 8.5 %collective-permute-start.10 = (f32[32,4,1,128]{3,0,2,1:T(8,128)}, f32[32,4,1,128]{3,0,2,1:T(8,128)S(1)}, u32[]{:S(2)}, u32[]{:S(2)}) collective-permute-start(f32[32,4,1,128]{3,0,2,1:T(8,128)} %get-tuple-element.239), channel_id=1, source_target_pairs={{8,0},{16,8},{24,16},{32,24},{40,32},{48,40},{56,48},{64,56},{72,6... | collective-permute-start | bytes 196616 | tf_op jit(solution)/shard_map/ppermute | solution.py:32
  345.9 7.0 collective-permute-start.11
  419.4 11.6 %collective-permute-start.16 = (f32[32,4,8,1]{3,0,2,1:T(8,128)S(1)}, f32[32,4,8,1]{3,0,2,1:T(8,128)S(1)}, u32[]{:S(2)}, u32[]{:S(2)}) collective-permute-start(f32[32,4,8,1]{3,0,2,1:T(8,128)S(1)} %get-tuple-element.230), channel_id=1, source_target_pairs={{1,0},{2,1},{3,2},{4,3},{5,4},{6,5},{7,6},{9,8},{10,9},{11,10},{12... | collective-permute-start | bytes 12296 | tf_op jit(solution)/shard_map/ppermute | solution.py:32
  421.5 9.6 %collective-permute-start.17 = (f32[32,4,8,1]{3,0,2,1:T(8,128)S(1)}, f32[32,4,8,1]{3,0,2,1:T(8,128)S(1)}, u32[]{:S(2)}, u32[]{:S(2)}) collective-permute-start(f32[32,4,8,1]{3,0,2,1:T(8,128)S(1)} %get-tuple-element.231), channel_id=1, source_target_pairs={{0,1},{1,2},{2,3},{3,4},{4,5},{5,6},{6,7},{8,9},{9,10},{10,11},{11... | collective-permute-start | bytes 12296 | tf_op jit(solution)/shard_map/ppermute | solution.py:31
  424.9 6.1 collective-permute-start.14
  426.2 5.6 collective-permute-start.15
  432.9 72.4 %copy-start.17 = (f32[4,8,8,128]{3,2,1,0:T(8,128)S(1)}, f32[4,8,8,128]{3,2,1,0:T(8,128)}, u32[]{:S(2)}) copy-start(f32[4,8,8,128]{3,2,1,0:T(8,128)} %copy.319) | copy-start | bytes 393220
  494.0 11.3 %collective-permute-start.20 = (f32[32,4,8,1]{3,0,2,1:T(8,128)S(1)}, f32[32,4,8,1]{3,0,2,1:T(8,128)S(1)}, u32[]{:S(2)}, u32[]{:S(2)}) collective-permute-start(f32[32,4,8,1]{3,0,2,1:T(8,128)S(1)} %get-tuple-element.224), channel_id=1, source_target_pairs={{1,0},{2,1},{3,2},{4,3},{5,4},{6,5},{7,6},{9,8},{10,9},{11,10},{12... | collective-permute-start | bytes 12296 | tf_op jit(solution)/shard_map/ppermute | solution.py:32
  496.1 9.6 %collective-permute-start.21 = (f32[32,4,8,1]{3,0,2,1:T(8,128)S(1)}, f32[32,4,8,1]{3,0,2,1:T(8,128)S(1)}, u32[]{:S(2)}, u32[]{:S(2)}) collective-permute-start(f32[32,4,8,1]{3,0,2,1:T(8,128)S(1)} %get-tuple-element.225), channel_id=1, source_target_pairs={{0,1},{1,2},{2,3},{3,4},{4,5},{5,6},{6,7},{8,9},{9,10},{10,11},{11... | collective-permute-start | bytes 12296 | tf_op jit(solution)/shard_map/ppermute | solution.py:31
  499.6 6.1 collective-permute-start.18
  500.9 5.6 collective-permute-start.19
  507.5 11.9 %collective-permute-start.24 = (f32[32,4,8,1]{3,0,2,1:T(8,128)S(1)}, f32[32,4,8,1]{3,0,2,1:T(8,128)S(1)}, u32[]{:S(2)}, u32[]{:S(2)}) collective-permute-start(f32[32,4,8,1]{3,0,2,1:T(8,128)S(1)} %get-tuple-element.218), channel_id=1, source_target_pairs={{1,0},{2,1},{3,2},{4,3},{5,4},{6,5},{7,6},{9,8},{10,9},{11,10},{12... | collective-permute-start | bytes 12296 | tf_op jit(solution)/shard_map/ppermute | solution.py:32
  509.5 9.9 %collective-permute-start.25 = (f32[32,4,8,1]{3,0,2,1:T(8,128)S(1)}, f32[32,4,8,1]{3,0,2,1:T(8,128)S(1)}, u32[]{:S(2)}, u32[]{:S(2)}) collective-permute-start(f32[32,4,8,1]{3,0,2,1:T(8,128)S(1)} %get-tuple-element.219), channel_id=1, source_target_pairs={{0,1},{1,2},{2,3},{3,4},{4,5},{5,6},{6,7},{8,9},{9,10},{10,11},{11... | collective-permute-start | bytes 12296 | tf_op jit(solution)/shard_map/ppermute | solution.py:31
  513.1 6.3 collective-permute-start.22
  514.4 6.0 collective-permute-start.23
  598.2 82.8 %copy-start.13 = (f32[32,32]{0,1:T(8,128)S(1)}, f32[32,32]{0,1:T(8,128)}, u32[]{:S(2)}) copy-start(f32[32,32]{0,1:T(8,128)} %copy-done.12) | copy-start | bytes 12292
  602.6 14.6 %collective-permute-start.28 = (f32[32,4,8,1]{3,0,2,1:T(8,128)}, f32[32,4,8,1]{3,0,2,1:T(8,128)S(1)}, u32[]{:S(2)}, u32[]{:S(2)}) collective-permute-start(f32[32,4,8,1]{3,0,2,1:T(8,128)} %get-tuple-element.212), channel_id=1, source_target_pairs={{1,0},{2,1},{3,2},{4,3},{5,4},{6,5},{7,6},{9,8},{10,9},{11,10},{12... | collective-permute-start | bytes 12296 | tf_op jit(solution)/shard_map/ppermute | solution.py:32
  604.7 12.5 %collective-permute-start.29 = (f32[32,4,8,1]{3,0,2,1:T(8,128)}, f32[32,4,8,1]{3,0,2,1:T(8,128)}, u32[]{:S(2)}, u32[]{:S(2)}) collective-permute-start(f32[32,4,8,1]{3,0,2,1:T(8,128)} %get-tuple-element.213), channel_id=1, source_target_pairs={{0,1},{1,2},{2,3},{3,4},{4,5},{5,6},{6,7},{8,9},{9,10},{10,11},{11... | collective-permute-start | bytes 12296 | tf_op jit(solution)/shard_map/ppermute | solution.py:31
  608.2 9.0 %collective-permute-start.26 = (f32[32,4,1,128]{3,0,2,1:T(8,128)}, f32[32,4,1,128]{3,0,2,1:T(8,128)S(1)}, u32[]{:S(2)}, u32[]{:S(2)}) collective-permute-start(f32[32,4,1,128]{3,0,2,1:T(8,128)} %get-tuple-element.215), channel_id=1, source_target_pairs={{8,0},{16,8},{24,16},{32,24},{40,32},{48,40},{56,48},{64,56},{72,6... | collective-permute-start | bytes 196616 | tf_op jit(solution)/shard_map/ppermute | solution.py:32
  609.5 7.7 %collective-permute-start.27 = (f32[32,4,1,128]{3,0,2,1:T(8,128)}, f32[32,4,1,128]{3,0,2,1:T(8,128)S(1)}, u32[]{:S(2)}, u32[]{:S(2)}) collective-permute-start(f32[32,4,1,128]{3,0,2,1:T(8,128)} %get-tuple-element.214), channel_id=1, source_target_pairs={{0,8},{8,16},{16,24},{24,32},{32,40},{40,48},{48,56},{56,64},{64,7... | collective-permute-start | bytes 196616 | tf_op jit(solution)/shard_map/ppermute | solution.py:31
  619.8 62.6 %copy-start.14 = (f32[32,32]{0,1:T(8,128)S(1)}, f32[32,32]{0,1:T(8,128)}, u32[]{:S(2)}) copy-start(f32[32,32]{0,1:T(8,128)} %copy-done.12) | copy-start | bytes 12292
  619.8 62.8 %copy-start.21 = (f32[1,32,32]{1,2,0:T(8,128)S(1)}, f32[1,32,32]{1,2,0:T(8,128)}, u32[]{:S(2)}) copy-start(f32[1,32,32]{1,2,0:T(8,128)} %custom-call.25) | copy-start | bytes 12292
  683.8 11.6 %collective-permute-start.32 = (f32[32,4,8,1]{3,0,2,1:T(8,128)S(1)}, f32[32,4,8,1]{3,0,2,1:T(8,128)S(1)}, u32[]{:S(2)}, u32[]{:S(2)}) collective-permute-start(f32[32,4,8,1]{3,0,2,1:T(8,128)S(1)} %get-tuple-element.206), channel_id=1, source_target_pairs={{1,0},{2,1},{3,2},{4,3},{5,4},{6,5},{7,6},{9,8},{10,9},{11,10},{12... | collective-permute-start | bytes 12296 | tf_op jit(solution)/shard_map/ppermute | solution.py:32
  686.0 9.6 %collective-permute-start.33 = (f32[32,4,8,1]{3,0,2,1:T(8,128)S(1)}, f32[32,4,8,1]{3,0,2,1:T(8,128)S(1)}, u32[]{:S(2)}, u32[]{:S(2)}) collective-permute-start(f32[32,4,8,1]{3,0,2,1:T(8,128)S(1)} %get-tuple-element.207), channel_id=1, source_target_pairs={{0,1},{1,2},{2,3},{3,4},{4,5},{5,6},{6,7},{8,9},{9,10},{10,11},{11... | collective-permute-start | bytes 12296 | tf_op jit(solution)/shard_map/ppermute | solution.py:31
  689.4 6.1 collective-permute-start.30
  690.7 5.6 collective-permute-start.31
  (17 other events, 172.8 us)
